TPU v7x, 128 devices: a whole 4x4x4 slice. The times are simulated.
128 devices in a mesh: row: 8 (over z, x_hi), col: 16 (over x_lo, y, core).
Axes of the slice: x: 4 (x_hi: 2, x_lo: 2; x = x_hi * 2 + x_lo), y: 4, z: 4, core: 2. Of those that a mesh axis runs over, the one named last changes fastest.
Arguments:
- embeddings: bfloat16 [32768, 768], P(('row', 'col'))
- spread: bfloat16 [32768], P(('row', 'col')), may hold values from 1 to 16
- features: bfloat16 [32768, 256], P(('row', 'col')), may hold values from -160 to 160
- block_list: int32 [256], replicated, may hold values from 0 to 63
- list_pairs: int32 [64, 64], replicated, may hold values from 0 to 1, as said below
Outputs:
- smoothed: float32 [32768, 256], P(('row', 'col'))
Inputs may be any that keep to these rules, and one draw needn't show every extreme that they name: `list_pairs`: symmetric, with ones on the diagonal.
All inputs are finite; a program needn't handle non-finite values.
Results may differ from a plain program's by a relative error of at most 0.0029.
Values may be sent and summed in bfloat16 or wider, within the bound.
A program may use at most 64 MiB of HBM per device.

v0:
```python
import math

import jax
import jax.numpy as jnp
from jax import lax
from jax.sharding import PartitionSpec as P

BLK = 128
LISTS = 64


def active_table(block_list, list_pairs, row_blocks, col_blocks):
    count = block_list.shape[0]
    lists_onehot = (block_list[:, None] == jnp.arange(LISTS, dtype=jnp.int32)[None, :]).astype(
        jnp.float32
    )
    pair_table = list_pairs.astype(jnp.float32)
    row_select = (row_blocks[:, None] == jnp.arange(count, dtype=jnp.int32)[None, :]).astype(
        jnp.float32
    )
    col_select = (col_blocks[:, None] == jnp.arange(count, dtype=jnp.int32)[None, :]).astype(
        jnp.float32
    )
    row_onehot = jnp.dot(row_select, lists_onehot, precision=lax.Precision.HIGHEST)
    col_onehot = jnp.dot(col_select, lists_onehot, precision=lax.Precision.HIGHEST)
    joined = jnp.dot(row_onehot, pair_table, precision=lax.Precision.HIGHEST)
    return jnp.dot(joined, col_onehot.T, precision=lax.Precision.HIGHEST)


def shards(embeddings, spread, features, block_list, list_pairs):
    rows_x, rows_beta = (
        lax.all_gather(embeddings, "col", axis=0, tiled=True),
        lax.all_gather(spread, "col", axis=0, tiled=True),
    )
    cols_x, cols_beta, cols_feat = (
        lax.all_gather(embeddings, "row", axis=0, tiled=True),
        lax.all_gather(spread, "row", axis=0, tiled=True),
        lax.all_gather(features, "row", axis=0, tiled=True),
    )
    own_count = embeddings.shape[0]
    col_size = lax.axis_size("col")
    row_index = lax.axis_index("row")
    col_index = lax.axis_index("col")
    total_rows = rows_x.shape[0]
    total_cols = cols_x.shape[0]
    row_ids = row_index * total_rows + jnp.arange(total_rows, dtype=jnp.int32)
    local_index = jnp.arange(total_cols, dtype=jnp.int32)
    col_ids = (
        local_index // own_count * col_size + col_index
    ) * own_count + local_index % own_count
    active = active_table(block_list, list_pairs, row_ids[::BLK] // BLK, col_ids[::BLK] // BLK)
    col_blocks = active.shape[1]
    row_norm = jnp.sum(jnp.square(rows_x.astype(jnp.float32)), axis=1)
    col_norm = jnp.sum(jnp.square(cols_x.astype(jnp.float32)), axis=1)
    row_bw = rows_beta.astype(jnp.float32)
    col_bw = cols_beta.astype(jnp.float32)

    def block_terms(start, size):
        row_emb = lax.dynamic_slice_in_dim(rows_x, start, size, 0)
        norm_part = lax.dynamic_slice_in_dim(row_norm, start, size, 0)
        beta_part = lax.dynamic_slice_in_dim(row_bw, start, size, 0)
        ids_part = lax.dynamic_slice_in_dim(row_ids, start, size, 0)
        inner = lax.dot_general(
            row_emb, cols_x, (((1,), (1,)), ((), ())), preferred_element_type=jnp.float32
        )
        dist = norm_part[:, None] + col_norm[None, :] - 2.0 * inner
        active_part = lax.dynamic_slice_in_dim(active, start // BLK, size // BLK, 0)
        expanded = jnp.broadcast_to(
            active_part[:, None, :, None], (size // BLK, BLK, col_blocks, BLK)
        )
        mask = expanded.reshape(size, total_cols) * (ids_part[:, None] != col_ids[None, :]).astype(
            jnp.float32
        )
        near = mask * jnp.exp(-beta_part[:, None] * dist)
        return (mask, dist, near)

    block_rows = math.gcd(total_rows, 512)
    starts = jnp.arange(total_rows // block_rows, dtype=jnp.int32) * block_rows
    row_partial = lax.map(
        lambda start: jnp.sum(block_terms(start, block_rows)[2], axis=1), starts
    ).reshape(total_rows)
    row_totals = lax.psum(row_partial, "col")
    own_totals = lax.dynamic_slice_in_dim(row_totals, col_index * own_count, own_count, 0)
    col_totals = lax.all_gather(own_totals, "row", axis=0, tiled=True)
    size = math.gcd(total_rows, 512)

    def one_block(begin):
        mask, dist, near = block_terms(begin, size)
        far = mask * jnp.exp(-col_bw[None, :] * dist)
        total_part = lax.dynamic_slice_in_dim(row_totals, begin, size, 0)
        weight = ((near / total_part[:, None] + far / col_totals[None, :]) * 0.5).astype(
            jnp.bfloat16
        )
        return jnp.dot(weight, cols_feat, preferred_element_type=jnp.float32)

    begins = 0 + jnp.arange(total_rows // size, dtype=jnp.int32) * size
    partial_out = lax.map(one_block, begins).reshape(total_rows, cols_feat.shape[1])
    summed = lax.psum(partial_out, "col")
    return lax.dynamic_slice_in_dim(summed, col_index * own_count, own_count, 0)


def solution(mesh):
    return jax.shard_map(
        shards,
        mesh=mesh,
        in_specs=(P(("row", "col"), None), P(("row", "col")), P(("row", "col"), None), P(), P()),
        out_specs=P(("row", "col"), None),
        check_vma=False,
    )
```

profile of v0, /device:TPU:1, one launch (start us, length us, event | category | flops | bytes accessed | tf_op | source)
XLA Modules:
  0.0 548.1 jit_solution(9659464464459559050)
XLA Ops:
  9.5 21.2 %all-gather = bf16[16,1,256]{2,1,0:T(2,128)(2,1)S(1)} all-gather(bf16[1,1,256]{2,1,0:T(2,128)(2,1)S(1)} %reshape.44), channel_id=1, replica_groups=mesh['row'=8,'col'=16] {'col'}, dimensions={0}, use_global_device_ids=true | all-gather | bytes 8704 | tf_op jit(solution)/shard_map/all_gather | solution.py:33
  30.6 20.6 %all-gather.1 = bf16[8,1,256]{2,1,0:T(2,128)(2,1)S(1)} all-gather(bf16[1,1,256]{2,1,0:T(2,128)(2,1)S(1)} %reshape.44), channel_id=1, replica_groups=mesh['row'=8,'col'=16] {'row'}, dimensions={0}, use_global_device_ids=true | all-gather | bytes 4608 | tf_op jit(solution)/shard_map/all_gather | solution.py:37
  54.4 21.0 %all-gather.9.cloned.1.call-done = bf16[2048,768]{1,0:T(8,128)(2,1)} async-done(((bf16[256,768]{1,0:T(8,128)(2,1)}), bf16[2048,768]{1,0:T(8,128)(2,1)}) %all-gather.9.cloned.1.call-update) | async-done | bytes 3145744 | tf_op jit(solution)/shard_map/all_gather | solution.py:36
  75.3 2.7 multiply_reduce_fusion.1
  78.1 39.8 %all-gather.7.cloned.1.call-done = bf16[4096,768]{1,0:T(8,128)(2,1)} async-done(((bf16[256,768]{1,0:T(8,128)(2,1)}), bf16[4096,768]{1,0:T(8,128)(2,1)}) %all-gather.7.cloned.1.call-update) | async-done | bytes 6291472 | tf_op jit(solution)/shard_map/all_gather | solution.py:32
  117.9 4.1 multiply_reduce_fusion
  122.0 102.0 %while.26 = (s32[]{:T(128)}, f32[8,512]{1,0:T(8,128)S(1)}, s32[8]{0:T(128)S(1)}, s32[4096]{0:T(1024)S(1)}, f32[32,16]{1,0:T(8,128)S(1)}, /*index=5*/f32[4096]{0:...) while((s32[]{:T(128)}, f32[8,512]{1,0:T(8,128)S(1)}, ...), condition=%wide.region_4.5_spmd.clone, body=%wide.region_2.4_spmd.clone.sunk | while | flops 1619034112 | bytes 12371102 | solution.py:79
  125.1 2.4 broadcast_in_dim.65
  129.0 5.8 %fusion.78 = f32[512]{0:T(512)S(1)} fusion(f32[64,8,16,128]{3,2,1,0:T(8,128)} %bitcast.66, bf16[2048,768]{1,0:T(8,128)(2,1)S(1)} %get-tuple-element.698, f32[2048]{0:T(1024)S(1)} %get-tuple-element.696, f32[512]{0:T(512)S(1)} %dynamic_slice.127, f32[512]{0:T(512)S(1)} %dynamic-slice_negate_fusion.4, s32[2048]{0:T(1024)S(1)} %fusion.77, ...), kind=kOutput, calls=%fused_computation.4.clone.1 | convolution fusion | flops 1619000832 | bytes 8151044 | tf_op jit(solution)/shard_map/while/body/eval_jaxpr/dot_general | solution.py:63
  137.9 2.4 broadcast_in_dim.65
  141.8 5.7 %fusion.78 = f32[512]{0:T(512)S(1)} fusion(f32[64,8,16,128]{3,2,1,0:T(8,128)} %bitcast.66, bf16[2048,768]{1,0:T(8,128)(2,1)S(1)} %get-tuple-element.698, f32[2048]{0:T(1024)S(1)} %get-tuple-element.696, f32[512]{0:T(512)S(1)} %dynamic_slice.127, f32[512]{0:T(512)S(1)} %dynamic-slice_negate_fusion.4, s32[2048]{0:T(1024)S(1)} %fusion.77, ...), kind=kOutput, calls=%fused_computation.4.clone.1 | convolution fusion | flops 1619000832 | bytes 8151044 | tf_op jit(solution)/shard_map/while/body/eval_jaxpr/dot_general | solution.py:63
  150.7 2.4 broadcast_in_dim.65
  154.6 5.7 %fusion.78 = f32[512]{0:T(512)S(1)} fusion(f32[64,8,16,128]{3,2,1,0:T(8,128)} %bitcast.66, bf16[2048,768]{1,0:T(8,128)(2,1)S(1)} %get-tuple-element.698, f32[2048]{0:T(1024)S(1)} %get-tuple-element.696, f32[512]{0:T(512)S(1)} %dynamic_slice.127, f32[512]{0:T(512)S(1)} %dynamic-slice_negate_fusion.4, s32[2048]{0:T(1024)S(1)} %fusion.77, ...), kind=kOutput, calls=%fused_computation.4.clone.1 | convolution fusion | flops 1619000832 | bytes 8151044 | tf_op jit(solution)/shard_map/while/body/eval_jaxpr/dot_general | solution.py:63
  163.4 2.4 broadcast_in_dim.65
  167.3 5.7 %fusion.78 = f32[512]{0:T(512)S(1)} fusion(f32[64,8,16,128]{3,2,1,0:T(8,128)} %bitcast.66, bf16[2048,768]{1,0:T(8,128)(2,1)S(1)} %get-tuple-element.698, f32[2048]{0:T(1024)S(1)} %get-tuple-element.696, f32[512]{0:T(512)S(1)} %dynamic_slice.127, f32[512]{0:T(512)S(1)} %dynamic-slice_negate_fusion.4, s32[2048]{0:T(1024)S(1)} %fusion.77, ...), kind=kOutput, calls=%fused_computation.4.clone.1 | convolution fusion | flops 1619000832 | bytes 8151044 | tf_op jit(solution)/shard_map/while/body/eval_jaxpr/dot_general | solution.py:63
  176.2 2.4 broadcast_in_dim.65
  180.1 5.7 %fusion.78 = f32[512]{0:T(512)S(1)} fusion(f32[64,8,16,128]{3,2,1,0:T(8,128)} %bitcast.66, bf16[2048,768]{1,0:T(8,128)(2,1)S(1)} %get-tuple-element.698, f32[2048]{0:T(1024)S(1)} %get-tuple-element.696, f32[512]{0:T(512)S(1)} %dynamic_slice.127, f32[512]{0:T(512)S(1)} %dynamic-slice_negate_fusion.4, s32[2048]{0:T(1024)S(1)} %fusion.77, ...), kind=kOutput, calls=%fused_computation.4.clone.1 | convolution fusion | flops 1619000832 | bytes 8151044 | tf_op jit(solution)/shard_map/while/body/eval_jaxpr/dot_general | solution.py:63
  192.8 5.7 %fusion.78 = f32[512]{0:T(512)S(1)} fusion(f32[64,8,16,128]{3,2,1,0:T(8,128)} %bitcast.66, bf16[2048,768]{1,0:T(8,128)(2,1)S(1)} %get-tuple-element.698, f32[2048]{0:T(1024)S(1)} %get-tuple-element.696, f32[512]{0:T(512)S(1)} %dynamic_slice.127, f32[512]{0:T(512)S(1)} %dynamic-slice_negate_fusion.4, s32[2048]{0:T(1024)S(1)} %fusion.77, ...), kind=kOutput, calls=%fused_computation.4.clone.1 | convolution fusion | flops 1619000832 | bytes 8151044 | tf_op jit(solution)/shard_map/while/body/eval_jaxpr/dot_general | solution.py:63
  205.5 5.7 %fusion.78 = f32[512]{0:T(512)S(1)} fusion(f32[64,8,16,128]{3,2,1,0:T(8,128)} %bitcast.66, bf16[2048,768]{1,0:T(8,128)(2,1)S(1)} %get-tuple-element.698, f32[2048]{0:T(1024)S(1)} %get-tuple-element.696, f32[512]{0:T(512)S(1)} %dynamic_slice.127, f32[512]{0:T(512)S(1)} %dynamic-slice_negate_fusion.4, s32[2048]{0:T(1024)S(1)} %fusion.77, ...), kind=kOutput, calls=%fused_computation.4.clone.1 | convolution fusion | flops 1619000832 | bytes 8151044 | tf_op jit(solution)/shard_map/while/body/eval_jaxpr/dot_general | solution.py:63
  218.3 5.7 %fusion.78 = f32[512]{0:T(512)S(1)} fusion(f32[64,8,16,128]{3,2,1,0:T(8,128)} %bitcast.66, bf16[2048,768]{1,0:T(8,128)(2,1)S(1)} %get-tuple-element.698, f32[2048]{0:T(1024)S(1)} %get-tuple-element.696, f32[512]{0:T(512)S(1)} %dynamic_slice.127, f32[512]{0:T(512)S(1)} %dynamic-slice_negate_fusion.4, s32[2048]{0:T(1024)S(1)} %fusion.77, ...), kind=kOutput, calls=%fused_computation.4.clone.1 | convolution fusion | flops 1619000832 | bytes 8151044 | tf_op jit(solution)/shard_map/while/body/eval_jaxpr/dot_general | solution.py:63
  224.0 51.3 %psum.14 = f32[4096]{0:T(1024)S(1)} all-reduce(f32[4096]{0:T(1024)S(1)} %bitcast.69), channel_id=1, replica_groups=mesh['row'=8,'col'=16] {'col'}, use_global_device_ids=true, to_apply=%region_5.6 | all-reduce | flops 4096 | bytes 32768 | tf_op jit(solution)/shard_map/psum | solution.py:82
  275.4 19.4 %all-gather.2 = f32[8,1,256]{2,1,0:T(1,128)S(1)} all-gather(f32[1,1,256]{2,1,0:T(1,128)S(1)} %bitcast.75), channel_id=1, replica_groups=mesh['row'=8,'col'=16] {'row'}, dimensions={0}, use_global_device_ids=true | all-gather | bytes 9216 | tf_op jit(solution)/shard_map/all_gather | solution.py:84
  294.8 114.9 %while.27 = (s32[]{:T(128)}, f32[8,512,256]{2,1,0:T(8,128)}, s32[8]{0:T(128)S(1)}, s32[4096]{0:T(1024)S(1)}, f32[32,16]{1,0:T(8,128)S(1)}, /*index=5*/f32[4096]{...) while((s32[]{:T(128)}, f32[8,512,256]{2,1,0:T(8,128)}, ...), condition=%wide.region_7.8_spmd.clone, body=%wide.region_6.7_spmd.clone.sunk | while | flops 2162196992 | bytes 13960894 | solution.py:97
  301.6 7.6 %fusion.83 = f32[8,512,256]{2,1,0:T(8,128)} fusion(f32[8,512,256]{2,1,0:T(8,128)} %get-tuple-element.730, s32[]{:T(128)} %get-tuple-element.729, bf16[2048,256]{1,0:T(8,128)(2,1)} %get-tuple-element.764, f32[64,8,16,128]{3,2,1,0:T(8,128)} %bitcast.65, bf16[2048,768]{1,0:T(8,128)(2,1)S(1)} %get-tuple-element.760, f32[2048]{0:T(1024)S(1)} %get-tuple-element.763, ...), kind=kOutput, calls=%fused_computation.28.clone.1 | convolution fusion | flops 2162163712 | bytes 9740804 | tf_op jit(solution)/shard_map/while/body/eval_jaxpr/dot_general | solution.py:94
  315.9 7.6 %fusion.83 = f32[8,512,256]{2,1,0:T(8,128)} fusion(f32[8,512,256]{2,1,0:T(8,128)} %get-tuple-element.730, s32[]{:T(128)} %get-tuple-element.729, bf16[2048,256]{1,0:T(8,128)(2,1)} %get-tuple-element.764, f32[64,8,16,128]{3,2,1,0:T(8,128)} %bitcast.65, bf16[2048,768]{1,0:T(8,128)(2,1)S(1)} %get-tuple-element.760, f32[2048]{0:T(1024)S(1)} %get-tuple-element.763, ...), kind=kOutput, calls=%fused_computation.28.clone.1 | convolution fusion | flops 2162163712 | bytes 9740804 | tf_op jit(solution)/shard_map/while/body/eval_jaxpr/dot_general | solution.py:94
  330.3 7.6 %fusion.83 = f32[8,512,256]{2,1,0:T(8,128)} fusion(f32[8,512,256]{2,1,0:T(8,128)} %get-tuple-element.730, s32[]{:T(128)} %get-tuple-element.729, bf16[2048,256]{1,0:T(8,128)(2,1)} %get-tuple-element.764, f32[64,8,16,128]{3,2,1,0:T(8,128)} %bitcast.65, bf16[2048,768]{1,0:T(8,128)(2,1)S(1)} %get-tuple-element.760, f32[2048]{0:T(1024)S(1)} %get-tuple-element.763, ...), kind=kOutput, calls=%fused_computation.28.clone.1 | convolution fusion | flops 2162163712 | bytes 9740804 | tf_op jit(solution)/shard_map/while/body/eval_jaxpr/dot_general | solution.py:94
  344.6 7.6 %fusion.83 = f32[8,512,256]{2,1,0:T(8,128)} fusion(f32[8,512,256]{2,1,0:T(8,128)} %get-tuple-element.730, s32[]{:T(128)} %get-tuple-element.729, bf16[2048,256]{1,0:T(8,128)(2,1)} %get-tuple-element.764, f32[64,8,16,128]{3,2,1,0:T(8,128)} %bitcast.65, bf16[2048,768]{1,0:T(8,128)(2,1)S(1)} %get-tuple-element.760, f32[2048]{0:T(1024)S(1)} %get-tuple-element.763, ...), kind=kOutput, calls=%fused_computation.28.clone.1 | convolution fusion | flops 2162163712 | bytes 9740804 | tf_op jit(solution)/shard_map/while/body/eval_jaxpr/dot_general | solution.py:94
  359.0 7.6 %fusion.83 = f32[8,512,256]{2,1,0:T(8,128)} fusion(f32[8,512,256]{2,1,0:T(8,128)} %get-tuple-element.730, s32[]{:T(128)} %get-tuple-element.729, bf16[2048,256]{1,0:T(8,128)(2,1)} %get-tuple-element.764, f32[64,8,16,128]{3,2,1,0:T(8,128)} %bitcast.65, bf16[2048,768]{1,0:T(8,128)(2,1)S(1)} %get-tuple-element.760, f32[2048]{0:T(1024)S(1)} %get-tuple-element.763, ...), kind=kOutput, calls=%fused_computation.28.clone.1 | convolution fusion | flops 2162163712 | bytes 9740804 | tf_op jit(solution)/shard_map/while/body/eval_jaxpr/dot_general | solution.py:94
  373.4 7.7 %fusion.83 = f32[8,512,256]{2,1,0:T(8,128)} fusion(f32[8,512,256]{2,1,0:T(8,128)} %get-tuple-element.730, s32[]{:T(128)} %get-tuple-element.729, bf16[2048,256]{1,0:T(8,128)(2,1)} %get-tuple-element.764, f32[64,8,16,128]{3,2,1,0:T(8,128)} %bitcast.65, bf16[2048,768]{1,0:T(8,128)(2,1)S(1)} %get-tuple-element.760, f32[2048]{0:T(1024)S(1)} %get-tuple-element.763, ...), kind=kOutput, calls=%fused_computation.28.clone.1 | convolution fusion | flops 2162163712 | bytes 9740804 | tf_op jit(solution)/shard_map/while/body/eval_jaxpr/dot_general | solution.py:94
  387.8 7.6 %fusion.83 = f32[8,512,256]{2,1,0:T(8,128)} fusion(f32[8,512,256]{2,1,0:T(8,128)} %get-tuple-element.730, s32[]{:T(128)} %get-tuple-element.729, bf16[2048,256]{1,0:T(8,128)(2,1)} %get-tuple-element.764, f32[64,8,16,128]{3,2,1,0:T(8,128)} %bitcast.65, bf16[2048,768]{1,0:T(8,128)(2,1)S(1)} %get-tuple-element.760, f32[2048]{0:T(1024)S(1)} %get-tuple-element.763, ...), kind=kOutput, calls=%fused_computation.28.clone.1 | convolution fusion | flops 2162163712 | bytes 9740804 | tf_op jit(solution)/shard_map/while/body/eval_jaxpr/dot_general | solution.py:94
  402.1 7.6 %fusion.83 = f32[8,512,256]{2,1,0:T(8,128)} fusion(f32[8,512,256]{2,1,0:T(8,128)} %get-tuple-element.730, s32[]{:T(128)} %get-tuple-element.729, bf16[2048,256]{1,0:T(8,128)(2,1)} %get-tuple-element.764, f32[64,8,16,128]{3,2,1,0:T(8,128)} %bitcast.65, bf16[2048,768]{1,0:T(8,128)(2,1)S(1)} %get-tuple-element.760, f32[2048]{0:T(1024)S(1)} %get-tuple-element.763, ...), kind=kOutput, calls=%fused_computation.28.clone.1 | convolution fusion | flops 2162163712 | bytes 9740804 | tf_op jit(solution)/shard_map/while/body/eval_jaxpr/dot_general | solution.py:94
  409.7 130.2 %all-reduce.2.cloned.1.call-done = f32[4096,256]{1,0:T(8,128)} async-done(((f32[4096,256]{1,0:T(8,128)}), f32[4096,256]{1,0:T(8,128)}) %all-reduce.2.cloned.1.call-update) | async-done | bytes 4194320 | tf_op jit(solution)/shard_map/psum | solution.py:98
  (153 shorter events, 48.5 us)
Async XLA Ops:
  6.5 68.8 %all-gather.9.cloned.1.call-start = ((), (), s32[]{:S(2)}) async-start(), calls=%async_computation.1 | async-start | bytes 3538944 | tf_op jit(solution)/shard_map/all_gather | solution.py:36
  7.3 110.6 %all-gather.7.cloned.1.call-start = ((), (), s32[]{:S(2)}) async-start(), calls=%async_computation | async-start | bytes 6684672 | tf_op jit(solution)/shard_map/all_gather | solution.py:32
  8.0 286.8 %all-gather.11.cloned.1.call-start = ((), (), s32[]{:S(2)}) async-start(), calls=%async_computation.2 | async-start | bytes 1179648 | tf_op jit(solution)/shard_map/all_gather | solution.py:38
  8.7 531.2 %all-reduce.2.cloned.1.call-start = ((), (), s32[]{:S(2)}) async-start(), calls=%async_computation.3 | async-start | bytes 8388608 | tf_op jit(solution)/shard_map/psum | solution.py:98
  75.3 46.6 %copy-start = (bf16[2048,768]{1,0:T(8,128)(2,1)S(1)}, bf16[2048,768]{1,0:T(8,128)(2,1)}, u32[]{:S(2)}) copy-start(bf16[2048,768]{1,0:T(8,128)(2,1)} %all-gather.9.cloned.1.call-done) | copy-start | bytes 9437188
Sparse Core Ops, SparseCore 0:
  9.7 65.6 all-gather.8
  77.0 40.7 all-gather.6
  120.2 45.7 all-gather.10
  409.9 130.0 all-reduce.1
where the time goes:
time: 549 us; the launch traced here: 548 us
  waiting for transfers between devices  193 us (35%)
  blocking collectives  112 us (20%)
  matrix products  109 us (20%)
  loops' own time  57.7 us (11%)
  local copies, waits for them, and re-layouts  54 us (10%)
  between operations  13.2 us (2%)
  other arithmetic  8.3 us (2%)
    psum x1, waiting for transfers between devices, shards(): summed = lax.psum(partial_out, 'col')  130 us
    dot_general x8, matrix products, one_block(): return jnp.dot(weight, cols_feat, preferred_element_type=jnp.float32)  61 us
    psum x1, blocking collectives, shards(): row_totals = lax.psum(row_partial, 'col')  51.3 us
    dot_general x8, matrix products, block_terms(): lax.dot_general(row_emb, cols_x, (((1,), (1,)), ((), ())), preferred_elem...  45.4 us
    all_gather x1, waiting for transfers between devices, shards(): lax.all_gather(embeddings, 'col', axis=0, tiled=True)  39.8 us
    broadcast_in_dim x16, local copies, waits for them, and re-layouts, block_terms(): jnp.broadcast_to(active_part[:, None, :, None], (size // BLK, BLK, col_bl...  38.6 us
    another operation x1, loops' own time, shards(): lax.map(lambda start: jnp.sum(block_terms(start, block_rows)[2], axis=1),...  30.1 us
    another operation x1, loops' own time, shards(): lax.map(one_block, begins).reshape(total_rows, cols_feat.shape[1])  27.6 us
  transfers between devices with their start and end apart: 4, of which 3 were waited for; matrix products, arithmetic and copies ran while one was open for 15% of the time, Pallas kernels for 0%

commit v1 on v0

v1 whole, which is shorter than its diff:
```python
import math

import jax
import jax.numpy as jnp
from jax import lax
from jax.experimental import pallas as pl
from jax.experimental.pallas import tpu as pltpu
from jax.sharding import PartitionSpec as P

BLK = 128
F32 = jnp.float32
BF16 = jnp.bfloat16
LOG2E = math.log2(math.e)
INF = float("inf")
MESH = pl.DeviceIdType.MESH

RECTS = (
    (0, 1, 0, 1),
    (1, 2, 0, 1),
    (0, 3, 1, 2),
    (3, 2, 0, 3),
    (0, 5, 3, 1),
    (0, 5, 4, 1),
    (5, 2, 0, 5),
    (7, 1, 0, 5),
    (0, 8, 5, 2),
    (0, 8, 7, 1),
)


def slot_of(pos):
    low = pos % 4
    return pos + (low == 2).astype(jnp.int32) - (low == 3).astype(jnp.int32)


def kernel(
    x_ref, xt_ref, f_ref, aux_ref, bl_ref, lp_ref, out_ref,
    rx, ct, fb, t_ref, rn, rc, ra, ca, cs, tr, al, ral, cal, cv, w_ref, sr, ob, obr, rl, cl,
    loc, rx_s, rx_r, dd_s, dd_r, ct_s, ct_r, fb_s, fb_r, ax_s, rax_r, cax_r, tr_s, tr_r,
    al_s, ral_r, cal_r, sr_s, sr_r, ob_s, ob_r,
):
    own = x_ref.shape[0]
    wide = x_ref.shape[1]
    half = own // 2
    row = lax.axis_index("row")
    col = lax.axis_index("col")
    xl, y, core = col // 8, (col // 2) % 4, col % 2
    z, xh = row // 2, row % 2

    def rpeer(dx, dy, dk):
        return {"col": ((xl + dx) % 2) * 8 + ((y + dy + 4) % 4) * 2 + (core + dk) % 2}

    def cpeer(dx, dz):
        return {"row": ((z + dz + 4) % 4) * 2 + (xh + dx) % 2}

    locals_ = [
        pltpu.make_async_copy(x_ref, rx.at[0, 0], loc.at[0]),
        pltpu.make_async_copy(xt_ref, ct.at[0], loc.at[1]),
        pltpu.make_async_copy(f_ref, fb.at[0], loc.at[2]),
        pltpu.make_async_copy(aux_ref, ra.at[0, 0], loc.at[3]),
        pltpu.make_async_copy(aux_ref, ca.at[0], loc.at[4]),
    ]
    for c in locals_:
        c.start()

    barrier = pltpu.get_barrier_semaphore()
    for i in range(8):
        for h in range(2):
            if i + h > 0:
                pl.semaphore_signal(
                    barrier, inc=1, device_id=rpeer(i // 4, i % 4, h), device_id_type=MESH
                )
        if i > 0:
            pl.semaphore_signal(barrier, inc=1, device_id=cpeer(i // 4, i % 4), device_id_type=MESH)

    for i in range(8):
        dx, e = i // 4, i % 4
        for h in range(2):
            owner = row * 16 + rpeer(dx, -e, h)["col"]
            for b in range(2):
                rl[i * 4 + h * 2 + b] = bl_ref[owner * 2 + b]
        owner = cpeer(dx, -e)["row"] * 16 + col
        for b in range(2):
            cl[i * 2 + b] = bl_ref[owner * 2 + b]
    cs[...] = jnp.zeros_like(cs)

    for c in locals_:
        c.wait()
    pl.semaphore_wait(barrier, 22)

    started = []

    def remote(src, dst, ssem, rsem, to):
        return pltpu.make_async_remote_copy(
            src_ref=src, dst_ref=dst, send_sem=ssem, recv_sem=rsem, device_id=to, device_id_type=MESH
        )

    def send(make):
        remote(*make()).start()
        started.append(make)

    def arrived(dst, rsem):
        pltpu.make_async_remote_copy(
            src_ref=dst, dst_ref=dst, send_sem=rsem, recv_sem=rsem,
            device_id=rpeer(0, 0, 1), device_id_type=MESH,
        ).wait_recv()

    class Gather:
        def __init__(self, view, ssem, rsem, peer, size):
            self.view, self.ssem, self.rsem, self.peer, self.size = view, ssem, rsem, peer, size

        def parts(self, slot):
            return (
                self.view(slot, 0, self.size // 2),
                self.view(slot, self.size // 2, self.size // 2),
            )

        def whole(self, slot):
            return self.view(slot, 0, self.size)

        def own_x(self):
            send(lambda: (self.whole(0), self.whole(4), self.ssem.at[0], self.rsem.at[4, 0], self.peer(1, 0)))

        def ring(self, base, m):
            send(lambda: (self.whole(base), self.whole(base + 1), self.ssem.at[m], self.rsem.at[base + 1, 0], self.peer(0, 1)))
            send(lambda: (self.whole(base), self.whole(base + 3), self.ssem.at[m + 1], self.rsem.at[base + 3, 0], self.peer(0, -1)))

        def recv(self, slot):
            if slot % 4 == 2:
                a, b = self.parts(slot)
                arrived(a, self.rsem.at[slot, 0])
                arrived(b, self.rsem.at[slot, 1])
            else:
                arrived(self.whole(slot), self.rsem.at[slot, 0])

        def halves(self, base, m):
            send(lambda: (self.parts(base + 1)[0], self.parts(base + 2)[0], self.ssem.at[m], self.rsem.at[base + 2, 0], self.peer(0, 1)))
            send(lambda: (self.parts(base + 3)[1], self.parts(base + 2)[1], self.ssem.at[m + 1], self.rsem.at[base + 2, 1], self.peer(0, -1)))

    rows = Gather(lambda s, lo, n: rx.at[s, 0, pl.ds(lo, n)], rx_s, rx_r, lambda dx, d: rpeer(dx, d, 0), own)
    cols = Gather(lambda s, lo, n: ct.at[s, pl.ds(lo, n)], ct_s, ct_r, cpeer, wide)
    feat = Gather(lambda s, lo, n: fb.at[s, pl.ds(lo, n)], fb_s, fb_r, cpeer, own)

    def sibling(slot):
        send(lambda: (rx.at[slot, 0], rx.at[slot, 1], dd_s.at[slot], dd_r.at[slot], rpeer(0, 0, 1)))

    def spread_out(src, rdst, cdst, ssem, rrecv, crecv):
        for i in range(8):
            dx, e = i // 4, i % 4
            for h in range(2):
                if i + h > 0:
                    send(lambda i=i, h=h, dx=dx, e=e: (src, rdst.at[i, h], ssem.at[i, h], rrecv.at[i, h], rpeer(dx, e, h)))
            if i > 0:
                send(lambda i=i, dx=dx, e=e: (src, cdst.at[i], ssem.at[i, 2], crecv.at[i], cpeer(dx, e)))

    def lanes(a8, k):
        return jnp.broadcast_to(jnp.transpose(a8)[:, k : k + 1], (own, 128))

    def row_terms(i, h):
        a8 = ra[i, h]
        rn[i, h * own : (h + 1) * own, :] = lanes(a8, 0)
        rc[i, h * own : (h + 1) * own, :] = lanes(a8, 1)

    def row_ready(i):
        for h in range(2):
            if i + h > 0:
                arrived(ra.at[i, h], rax_r.at[i, h])
            row_terms(i, h)
        arrived(rx.at[i, 1], dd_r.at[i])

    def col_ready(i):
        if i > 0:
            arrived(ca.at[i], cax_r.at[i])

    def pair(i, q, diagonal):
        lhs = rx[i].reshape(2 * own, wide)
        s = jnp.dot(lhs, ct[q], preferred_element_type=F32)
        acc0 = jnp.zeros((8, BLK), F32)
        acc = [acc0, acc0]
        for b in range(2 * own // BLK):
            base = []
            for cb in range(own // BLK):
                on = lp_ref[rl[i * 4 + b], cl[q * 2 + cb]]
                pen = jnp.where(on > 0, 0.0, INF).astype(F32)
                base.append(ca[q, 0:1, cb * BLK : (cb + 1) * BLK] + pen)
            for r8 in range(BLK // 8):
                lo = b * BLK + r8 * 8
                r_n = rn[i, lo : lo + 8, :]
                for cb in range(own // BLK):
                    d = (r_n + base[cb]) - s[lo : lo + 8, cb * BLK : (cb + 1) * BLK]
                    if diagonal and b == cb:
                        at_r = r8 * 8 + lax.broadcasted_iota(jnp.int32, (8, BLK), 0)
                        at_c = lax.broadcasted_iota(jnp.int32, (8, BLK), 1)
                        d = jnp.where(at_r == at_c, INF, d)
                    t_ref[i, lo : lo + 8, pl.ds(pl.multiple_of(q * own + cb * BLK, BLK), BLK)] = d
                    acc[cb] = acc[cb] + jnp.exp2(d * ca[q, 1:2, cb * BLK : (cb + 1) * BLK])
        cs[q] = cs[q] + jnp.concatenate(acc, axis=1)

    rows.ring(0, 1)
    cols.ring(0, 1)
    cols.own_x()
    rows.own_x()
    sibling(0)
    spread_out(aux_ref, ra, ca, ax_s, rax_r, cax_r)

    row_ready(0)
    pair(0, 0, True)

    def before(k):
        if k == 1:
            for s in (1, 3):
                rows.recv(s)
            rows.halves(0, 3)
            rows.recv(4)
            rows.ring(4, 5)
            for s in (1, 3):
                cols.recv(s)
            cols.halves(0, 3)
            for s in (1, 3, 4):
                sibling(s)
            for s in (1, 3):
                row_ready(s)
                col_ready(s)
        if k == 3:
            rows.recv(2)
            sibling(2)
            row_ready(4)
            row_ready(2)
        if k == 4:
            cols.recv(2)
            col_ready(2)
            feat.ring(0, 1)
        if k == 5:
            cols.recv(4)
            cols.ring(4, 5)
            col_ready(4)
            feat.own_x()
        if k == 6:
            for s in (5, 7):
                rows.recv(s)
            rows.halves(4, 7)
            for s in (5, 7):
                sibling(s)
            for s in (5, 7):
                row_ready(s)
        if k == 7:
            rows.recv(6)
            sibling(6)
            row_ready(6)
        if k == 8:
            for s in (5, 7):
                cols.recv(s)
            cols.halves(4, 7)
            for s in (1, 3):
                feat.recv(s)
            feat.halves(0, 3)
            feat.recv(4)
            feat.ring(4, 5)
            for s in (5, 7):
                col_ready(s)
        if k == 9:
            cols.recv(6)
            col_ready(6)

    def rect(k, carry):
        here = [(k == j).astype(jnp.int32) for j in range(1, len(RECTS))]
        first, count_r, lead, count_c = (
            sum(m * r[f] for m, r in zip(here, RECTS[1:])) for f in range(4)
        )
        for j in range(1, len(RECTS)):
            @pl.when(k == j)
            def _():
                before(j)

        def inner_c(cc, carry2):
            q = slot_of(lead + cc)

            def inner_r(rr, carry3):
                pair(slot_of(first + rr), q, False)
                return carry3

            return lax.fori_loop(0, count_r, inner_r, carry2)

        return lax.fori_loop(0, count_c, inner_c, carry)

    lax.fori_loop(1, len(RECTS), rect, 0)

    for q in range(1, 8):
        send(lambda q=q: (cs.at[q], tr.at[(q // 4) * 4 + (4 - q % 4) % 4], tr_s.at[q], tr_r.at[(q // 4) * 4 + (4 - q % 4) % 4], cpeer(q // 4, -(q % 4))))
    for s in (5, 7):
        feat.recv(s)
    feat.halves(4, 7)
    total = cs[0]
    for q in range(1, 8):
        arrived(tr.at[q], tr_r.at[q])
        total = total + tr[q]
    al[...] = jnp.broadcast_to(0.5 / jnp.sum(total, axis=0, keepdims=True), al.shape)
    ral[0, 0] = al[...]
    cal[0] = al[...]
    spread_out(al, ral, cal, al_s, ral_r, cal_r)
    for q in range(8):
        if q > 0:
            arrived(cal.at[q], cal_r.at[q])
        cv[0:1, q * own : (q + 1) * own] = ca[q, 1:2, :]
        cv[1:2, q * own : (q + 1) * own] = cal[q, 0:1, :]
    for i in range(8):
        for h in range(2):
            if i + h > 0:
                arrived(ral.at[i, h], ral_r.at[i, h])
    for s in (2, 6):
        feat.recv(s)

    total_cols = 8 * own
    step_r, step_c = 64, 256

    def weigh(i, h):
        ar = jnp.transpose(ral[i, h])[:, 0:1]
        for r in range(own // step_r):
            a_r = jnp.broadcast_to(ar[r * step_r : (r + 1) * step_r], (step_r, 128))
            a_r = jnp.concatenate([a_r] * (step_c // 128), axis=1)
            c_r = rc[i, h * own + r * step_r : h * own + (r + 1) * step_r, :]
            c_r = jnp.concatenate([c_r] * (step_c // 128), axis=1)
            for c in range(total_cols // step_c):
                sl = slice(c * step_c, (c + 1) * step_c)
                d = t_ref[i, h * own + r * step_r : h * own + (r + 1) * step_r, sl]
                v = jnp.exp2(d * c_r) * a_r + jnp.exp2(d * cv[0:1, sl]) * cv[1:2, sl]
                w_ref[h, r * step_r : (r + 1) * step_r, sl] = v.astype(BF16)

    def back(slot):
        return slot - slot % 4 + (4 - slot % 4) % 4

    def out_step(j, carry):
        i = slot_of(7 - j)
        dx, e = i // 4, i % 4
        feats = fb[...].reshape(total_cols, fb.shape[2])
        weigh(i, 1)
        other = jnp.dot(w_ref[1], feats, preferred_element_type=F32)
        t_ref[i, own : 2 * own, 0 : fb.shape[2]] = other
        pltpu.make_async_remote_copy(
            src_ref=t_ref.at[i, pl.ds(own, own), pl.ds(0, fb.shape[2])], dst_ref=sr.at[i],
            send_sem=sr_s.at[i], recv_sem=sr_r.at[i], device_id=rpeer(0, 0, 1), device_id_type=MESH,
        ).start()
        weigh(i, 0)
        mine = jnp.dot(w_ref[0], feats, preferred_element_type=F32)
        arrived(sr.at[i], sr_r.at[i])
        sr[i] = sr[i] + mine

        @pl.when(j < 7)
        def _():
            ob[i] = sr[i].astype(BF16)
            pltpu.make_async_remote_copy(
                src_ref=ob.at[i], dst_ref=obr.at[back(i)], send_sem=ob_s.at[i], recv_sem=ob_r.at[back(i)],
                device_id=rpeer(dx, 4 - e, 0), device_id_type=MESH,
            ).start()
        return carry

    lax.fori_loop(0, 8, out_step, 0)
    result = sr[0]
    for i in range(1, 8):
        arrived(obr.at[i], ob_r.at[i])
        result = result + obr[i].astype(F32)
    out_ref[...] = result
    for make in started:
        remote(*make()).wait_send()
    for i in range(8):
        pltpu.make_async_remote_copy(
            src_ref=t_ref.at[i, pl.ds(own, own), pl.ds(0, fb.shape[2])], dst_ref=sr.at[i],
            send_sem=sr_s.at[i], recv_sem=sr_r.at[i], device_id=rpeer(0, 0, 1), device_id_type=MESH,
        ).wait_send()
        if i > 0:
            pltpu.make_async_remote_copy(
                src_ref=ob.at[i], dst_ref=obr.at[i], send_sem=ob_s.at[i], recv_sem=ob_r.at[i],
                device_id=rpeer(0, 0, 1), device_id_type=MESH,
            ).wait_send()


def shards(embeddings, spread, features, block_list, list_pairs):
    own, wide = embeddings.shape
    feats = features.shape[1]
    norm = jnp.sum(jnp.square(embeddings.astype(F32)), axis=1)
    rate = spread.astype(F32) * (-LOG2E)
    aux = jnp.concatenate([norm[None], rate[None], jnp.zeros((6, own), F32)], axis=0)
    twice = (embeddings * jnp.asarray(2.0, BF16)).T
    anywhere = pl.BlockSpec(memory_space=pl.ANY)
    scalars = pl.BlockSpec(memory_space=pltpu.SMEM)
    vmem, dma = pltpu.VMEM, pltpu.SemaphoreType.DMA
    return pl.pallas_call(
        kernel,
        out_shape=jax.ShapeDtypeStruct((own, feats), F32),
        in_specs=[anywhere] * 4 + [scalars] * 2,
        out_specs=pl.BlockSpec(memory_space=pltpu.VMEM),
        scratch_shapes=[
            vmem((8, 2, own, wide), BF16),
            vmem((8, wide, own), BF16),
            vmem((8, own, feats), BF16),
            vmem((8, 2 * own, 8 * own), F32),
            vmem((8, 2 * own, 128), F32),
            vmem((8, 2 * own, 128), F32),
            vmem((8, 2, 8, own), F32),
            vmem((8, 8, own), F32),
            vmem((8, 8, own), F32),
            vmem((8, 8, own), F32),
            vmem((8, own), F32),
            vmem((8, 2, 8, own), F32),
            vmem((8, 8, own), F32),
            vmem((8, 8 * own), F32),
            vmem((2, own, 8 * own), BF16),
            vmem((8, own, feats), F32),
            vmem((8, own, feats), BF16),
            vmem((8, own, feats), BF16),
            pltpu.SMEM((32,), jnp.int32),
            pltpu.SMEM((16,), jnp.int32),
            dma((5,)),
            dma((9,)), dma((8, 2)), dma((8,)), dma((8,)),
            dma((9,)), dma((8, 2)), dma((9,)), dma((8, 2)),
            dma((8, 3)), dma((8, 2)), dma((8,)),
            dma((8,)), dma((8,)),
            dma((8, 3)), dma((8, 2)), dma((8,)),
            dma((8,)), dma((8,)), dma((8,)), dma((8,)),
        ],
        compiler_params=pltpu.CompilerParams(
            collective_id=0, has_side_effects=True, vmem_limit_bytes=60 * 2**20
        ),
        name="affinities",
    )(embeddings, twice, features, aux, block_list, list_pairs)


def solution(mesh):
    return jax.shard_map(
        shards,
        mesh=mesh,
        in_specs=(P(("row", "col"), None), P(("row", "col")), P(("row", "col"), None), P(), P()),
        out_specs=P(("row", "col"), None),
        check_vma=False,
    )
```

time: 549 us -> 101 us (0.18)
  waiting for transfers between devices: 193 us -> 0 us
  blocking collectives: 112 us -> 0 us
  matrix products: 109 us -> 0 us
  Pallas kernels: 0 us -> 95.8 us
  loops' own time: 57.7 us -> 0 us
  local copies, waits for them, and re-layouts: 54 us -> 1.92 us
  between operations: 13.2 us -> 0.02 us
    psum x1 -> x0, waiting for transfers between devices: 130 us -> none  [shards(): summed = lax.psum(partial_out, 'col')]
    dot_general x20 -> x0, matrix products: 109 us -> none  [the longest x8 61 us: one_block(): return jnp.dot(weight, cols_feat, preferred_element_type=jnp.float32)]
    pallas_call x0 -> x1, Pallas kernels: none -> 95.8 us  [shards(): pl.pallas_call(kernel, out_shape=jax.ShapeDtypeStruct((own, feats), F32),...]
    all_gather x3 -> x0, blocking collectives: 61.1 us -> none  [the longest x1 21.2 us: shards(): lax.all_gather(spread, 'col', axis=0, tiled=True)]
    all_gather x3 -> x0, waiting for transfers between devices: 60.8 us -> none  [the longest x1 39.8 us: shards(): lax.all_gather(embeddings, 'col', axis=0, tiled=True)]
    another operation x2 -> x0, loops' own time: 57.7 us -> none  [the longest x1 30.1 us: shards(): lax.map(lambda start: jnp.sum(block_terms(start, block_rows)[2], axis=1),...]
    psum x1 -> x0, blocking collectives: 51.3 us -> none  [shards(): row_totals = lax.psum(row_partial, 'col')]
    broadcast_in_dim x16 -> x1, local copies, waits for them, and re-layouts: 38.6 us -> 0.01 us  [shards(): jnp.zeros((6, own), F32)]
  transfers between devices with their start and end apart: 4 -> 0, of which waited for: 3 -> 0; matrix products, arithmetic and copies ran while one was open for 15% -> 0% of each run, Pallas kernels for 0% -> 0%
where the time goes in v1:
time: 101 us
  Pallas kernels  95.8 us (95%)
  other arithmetic  3.28 us (3%)
  local copies, waits for them, and re-layouts  1.92 us (2%)
    pallas_call x1, Pallas kernels, shards(): pl.pallas_call(kernel, out_shape=jax.ShapeDtypeStruct((own, feats), F32),...  95.8 us

profile of v1, /device:TPU:1, one launch (start us, length us, event | category | flops | bytes accessed | tf_op | source)
XLA Modules:
  0.0 101.0 jit_solution(9846078179356639587)
XLA Ops:
  0.0 0.0 copy-start
  0.0 0.1 pad.2.clone
  0.1 0.7 convert_multiply_fusion
  0.8 1.2 %multiply_reduce_fusion = f32[256]{0:T(256)S(1)} fusion(bf16[256,768]{1,0:T(8,128)(2,1)} %x_ref.1), kind=kLoop, calls=%fused_computation | loop fusion | flops 589568 | bytes 394240 | tf_op jit(solution)/shard_map/reduce_sum | solution.py:380
  1.9 0.7 maximum_maximum_fusion.aux_ref
  2.6 0.0 copy-done
  2.6 0.2 copy.6
  2.8 0.8 multiply_bitcast_fusion.xt_ref
  3.5 95.8 %affinities.1 = f32[256,256]{1,0:T(8,128)} custom-call(bf16[256,768]{1,0:T(8,128)(2,1)} %x_ref.1, bf16[768,256]{1,0:T(8,128)(2,1)} %multiply_bitcast_fusion.xt_ref, bf16[256,256]{1,0:T(8,128)(2,1)} %f_ref.1, f32[8,256]{1,0:T(8,128)} %maximum_maximum_fusion.aux_ref, s32[256]{0:T(256)} %bl_ref.1, s32[64,64]{1,0:T(8,128)} %lp_ref.1), custom_call_target="tpu_custom_call" | custom-call | tf_op jit(solution)/shard_map/affinities/pallas_call | solution.py:387
  99.3 1.7 %copy.8 = f32[256,256]{1,0:T(8,128)} copy(f32[256,256]{1,0:T(8,128)} %affinities.1) | data formatting | bytes 524288
  (1 shorter events, 0.0 us)
Async XLA Ops:
  0.0 2.6 %copy-start = (bf16[256,768]{1,0:T(8,128)(2,1)S(1)}, bf16[256,768]{1,0:T(8,128)(2,1)}, u32[]{:S(2)}) copy-start(bf16[256,768]{1,0:T(8,128)(2,1)} %x_ref.1) | copy-start | bytes 1179652

commit v2 on v0

v2 whole, which is shorter than its diff:
```python
import math

import jax
import jax.numpy as jnp
from jax import lax
from jax.experimental import pallas as pl
from jax.experimental.pallas import tpu as pltpu
from jax.sharding import PartitionSpec as P

BLK = 128
F32 = jnp.float32
BF16 = jnp.bfloat16
LOG2E = math.log2(math.e)
INF = float("inf")
MESH = pl.DeviceIdType.MESH

PLACES = ((0, 0), (1, 0), (0, 1), (0, 3), (1, 1), (1, 3), (0, 2), (1, 2))
SLOT = {p: s for s, p in enumerate(PLACES)}
BACK = [SLOT[(dx, (4 - e) % 4)] for dx, e in PLACES]
RECTS = ((0, 2, 0, 2), (2, 1, 0, 2), (0, 3, 2, 1), (3, 1, 0, 3), (0, 4, 3, 1))


def pick(i, values):
    return sum((i == s).astype(jnp.int32) * v for s, v in enumerate(values) if v)


def kernel(
    x_ref, f_ref, rate_ref, bl_ref, lp_ref, out_ref,
    rx, cx, fb, t_ref, rn, rc, ra, ca, cs, tr, al, ral, cal, cv, w0, w1, mn, sr, ob, obr, rl, cl,
    loc, rx_s, rx_r, dd_s, dd_r, cx_s, cx_r, fb_s, fb_r, tr_s, tr_r,
    al_s, ral_r, cal_r, sr_s, sr_r, ob_s, ob_r,
):
    own, wide = x_ref.shape
    feats = f_ref.shape[1]
    every = 8 * own
    row = lax.axis_index("row")
    col = lax.axis_index("col")
    xl, y, core = col // 8, (col // 2) % 4, col % 2
    z, xh = row // 2, row % 2

    def rpeer(dx, dy, dk):
        return {"col": ((xl + dx) % 2) * 8 + ((y + dy + 4) % 4) * 2 + (core + dk) % 2}

    def cpeer(dx, dz):
        return {
            "row": ((z + dz + 4) % 4) * 2 + (xh + dx) % 2,
            "col": ((xl + dx) % 2) * 8 + y * 2 + core,
        }

    barrier = pltpu.get_barrier_semaphore()
    met = [rpeer(0, 0, 1), rpeer(1, 0, 0), rpeer(0, 1, 0), rpeer(0, -1, 0)]
    met += [cpeer(1, 0), cpeer(0, 1), cpeer(0, -1)]
    for to in met:
        pl.semaphore_signal(barrier, inc=1, device_id=to, device_id_type=MESH)

    locals_ = [
        pltpu.make_async_copy(x_ref, rx.at[0, 0], loc.at[0]),
        pltpu.make_async_copy(x_ref, cx.at[0], loc.at[1]),
        pltpu.make_async_copy(f_ref, fb.at[0], loc.at[2]),
    ]
    for c in locals_:
        c.start()

    for i, (dx, e) in enumerate(PLACES):
        for h in range(2):
            owner = row * 16 + rpeer(dx, -e, h)["col"]
            for b in range(2):
                rl[i * 4 + h * 2 + b] = bl_ref[owner * 2 + b]
        owner = cpeer(dx, -e)["row"] * 16 + cpeer(dx, -e)["col"]
        for b in range(2):
            cl[i * 2 + b] = bl_ref[owner * 2 + b]
    cs[...] = jnp.zeros_like(cs)
    w0[...] = jnp.zeros_like(w0)

    for c in locals_:
        c.wait()
    xf = rx[0, 0].astype(F32)
    norm = jnp.sum(xf * xf, axis=1, keepdims=True) * 0.5
    norm = jnp.transpose(jnp.broadcast_to(norm, (own, 128)))
    ra[0, 0, 0:1, :] = norm[0:1, :]
    ra[0, 0, 1:8, :] = rate_ref[1:8, :]
    ca[0] = ra[0, 0]

    pl.semaphore_wait(barrier, len(met))

    started = []

    def remote(src, dst, ssem, rsem, to):
        return pltpu.make_async_remote_copy(
            src_ref=src, dst_ref=dst, send_sem=ssem, recv_sem=rsem, device_id=to, device_id_type=MESH
        )

    def send(make):
        remote(*make()).start()
        started.append(make)

    def arrived(dst, rsem):
        remote(dst, dst, rsem, rsem, rpeer(0, 0, 1)).wait_recv()

    class Gather:
        def __init__(self, view, side, ssem, rsem, peer, size):
            self.view, self.side, self.peer, self.size = view, side, peer, size
            self.ssem, self.rsem = ssem, rsem

        def move(self, m, a, b, part, to):
            n = self.size if part is None else self.size // 2
            lo = self.size // 2 if part == 1 else 0
            send(lambda: (self.view(a, lo, n), self.view(b, lo, n), self.ssem.at[m, 0], self.rsem.at[b, part or 0], self.peer(*to)))
            if self.side is not None and part != 1:
                send(lambda: (self.side(a), self.side(b), self.ssem.at[m, 1], self.rsem.at[b, 2], self.peer(*to)))

        def own_x(self):
            self.move(0, 0, 1, None, (1, 0))

        def ring(self, dx):
            base = SLOT[(dx, 0)]
            self.move(1 + 4 * dx, base, SLOT[(dx, 1)], None, (0, 1))
            self.move(2 + 4 * dx, base, SLOT[(dx, 3)], None, (0, -1))

        def halves(self, dx):
            self.move(3 + 4 * dx, SLOT[(dx, 1)], SLOT[(dx, 2)], 0, (0, 1))
            self.move(4 + 4 * dx, SLOT[(dx, 3)], SLOT[(dx, 2)], 1, (0, -1))

        def recv(self, slot):
            if PLACES[slot][1] == 2:
                n = self.size // 2
                arrived(self.view(slot, 0, n), self.rsem.at[slot, 0])
                arrived(self.view(slot, n, n), self.rsem.at[slot, 1])
            else:
                arrived(self.view(slot, 0, self.size), self.rsem.at[slot, 0])
            if self.side is not None:
                arrived(self.side(slot), self.rsem.at[slot, 2])

    rows = Gather(lambda s, lo, n: rx.at[s, 0, pl.ds(lo, n)], lambda s: ra.at[s, 0], rx_s, rx_r, lambda dx, d: rpeer(dx, d, 0), own)
    cols = Gather(lambda s, lo, n: cx.at[s, pl.ds(lo, n)], lambda s: ca.at[s], cx_s, cx_r, cpeer, own)
    feat = Gather(lambda s, lo, n: fb.at[s, pl.ds(lo, n)], None, fb_s, fb_r, cpeer, own)

    def sibling(slot):
        send(lambda: (rx.at[slot, 0], rx.at[slot, 1], dd_s.at[slot, 0], dd_r.at[slot, 0], rpeer(0, 0, 1)))
        send(lambda: (ra.at[slot, 0], ra.at[slot, 1], dd_s.at[slot, 1], dd_r.at[slot, 1], rpeer(0, 0, 1)))

    def lanes(a8, k):
        return jnp.broadcast_to(jnp.transpose(a8)[:, k : k + 1], (own, 128))

    def row_terms(i, h):
        rn[i, h * own : (h + 1) * own, :] = lanes(ra[i, h], 0)
        rc[i, h * own : (h + 1) * own, :] = lanes(ra[i, h], 1)

    def row_ready(i):
        row_terms(i, 0)
        arrived(rx.at[i, 1], dd_r.at[i, 0])
        arrived(ra.at[i, 1], dd_r.at[i, 1])
        row_terms(i, 1)

    def pair(ri, qi):
        m, n = 4 * own, 2 * own
        lhs = rx[pl.ds(2 * ri, 2)].reshape(m, wide)
        rhs = cx[pl.ds(2 * qi, 2)].reshape(n, wide)
        s = lax.dot_general(lhs, rhs, (((1,), (1,)), ((), ())), preferred_element_type=F32)
        self_pen = jnp.where(ri + qi == 0, INF, 0.0).astype(F32)
        acc = [jnp.zeros((8, BLK), F32) for _ in range(n // BLK)]
        per = own // BLK
        for b in range(m // BLK):
            base = []
            for cb in range(n // BLK):
                on = lp_ref[rl[ri * (m // BLK) + b], cl[qi * (n // BLK) + cb]]
                pen = jnp.where(on > 0, 0.0, INF).astype(F32)
                base.append(ca[2 * qi + cb // per, 0:1, (cb % per) * BLK : (cb % per + 1) * BLK] + pen)
            for r8 in range(BLK // 8):
                lo = b * BLK + r8 * 8
                at = (2 * ri + lo // (2 * own), slice(lo % (2 * own), lo % (2 * own) + 8))
                r_n = rn[at[0], at[1], :]
                for cb in range(n // BLK):
                    d = (r_n + base[cb]) - s[lo : lo + 8, cb * BLK : (cb + 1) * BLK]
                    if b == cb and b < per:
                        at_r = r8 * 8 + lax.broadcasted_iota(jnp.int32, (8, BLK), 0)
                        at_c = lax.broadcasted_iota(jnp.int32, (8, BLK), 1)
                        d = d + jnp.where(at_r == at_c, self_pen, 0.0)
                    t_ref[at[0], at[1], pl.ds(pl.multiple_of(qi * n + cb * BLK, BLK), BLK)] = d
                    rate = ca[2 * qi + cb // per, 1:2, (cb % per) * BLK : (cb % per + 1) * BLK]
                    acc[cb] = acc[cb] + jnp.exp2(d * rate)
        for c in range(2):
            cs[2 * qi + c] = cs[2 * qi + c] + jnp.concatenate(acc[c * per : (c + 1) * per], axis=1)

    def give_sum(q):
        dx, e = PLACES[q]
        send(lambda: (cs.at[q], tr.at[BACK[q]], tr_s.at[q], tr_r.at[BACK[q]], cpeer(dx, -e)))

    rows.ring(0)
    cols.ring(0)
    rows.own_x()
    cols.own_x()
    sibling(0)
    row_ready(0)

    def before(k):
        if k == 0:
            for g in (rows, cols):
                g.recv(1)
                g.ring(1)
                g.recv(2)
                g.recv(3)
                g.halves(0)
            for s in (1, 2, 3):
                sibling(s)
            for s in (1, 2, 3):
                row_ready(s)
        if k == 1:
            for g in (rows, cols):
                g.recv(4)
                g.recv(5)
                g.halves(1)
            for s in (4, 5):
                sibling(s)
            feat.ring(0)
            feat.own_x()
            for s in (4, 5):
                row_ready(s)
        if k == 3:
            for s in (6, 7):
                rows.recv(s)
                sibling(s)
            for s in (6, 7):
                row_ready(s)
        if k == 4:
            for s in (6, 7):
                cols.recv(s)
            for q in range(1, 6):
                give_sum(q)
            feat.recv(1)
            feat.ring(1)
            feat.recv(2)
            feat.recv(3)
            feat.halves(0)

    def rect(k, carry):
        first, count_r, lead, count_c = (pick(k, [r[f] for r in RECTS]) for f in range(4))
        for j in (0, 1, 3, 4):
            @pl.when(k == j)
            def _():
                before(j)

        def inner_c(cc, carry2):
            def inner_r(rr, carry3):
                pair(first + rr, lead + cc)
                return carry3

            return lax.fori_loop(0, count_r, inner_r, carry2)

        return lax.fori_loop(0, count_c, inner_c, carry)

    lax.fori_loop(0, len(RECTS), rect, 0)

    give_sum(6)
    give_sum(7)
    feat.recv(4)
    feat.recv(5)
    feat.halves(1)
    total = cs[0]
    for q in range(1, 8):
        arrived(tr.at[q], tr_r.at[q])
        total = total + tr[q]
    al[...] = jnp.broadcast_to(0.5 / jnp.sum(total, axis=0, keepdims=True), al.shape)
    ral[0, 0] = al[...]
    cal[0] = al[...]
    for i in (7, 6, 5, 4, 1, 3, 2, 0):
        dx, e = PLACES[i]
        if i > 0:
            send(lambda i=i, dx=dx, e=e: (al, cal.at[i], al_s.at[i, 2], cal_r.at[i], cpeer(dx, e)))
    for i in (7, 6, 5, 4, 1, 3, 2, 0):
        dx, e = PLACES[i]
        for h in (1, 0):
            if i + h > 0:
                send(lambda i=i, h=h, dx=dx, e=e: (al, ral.at[i, h], al_s.at[i, h], ral_r.at[i, h], rpeer(dx, e, h)))
    for q in range(8):
        if q > 0:
            arrived(cal.at[q], cal_r.at[q])
        cv[0:1, q * own : (q + 1) * own] = ca[q, 1:2, :]
        cv[1:2, q * own : (q + 1) * own] = cal[q, 0:1, :]

    feat.recv(6)
    feat.recv(7)
    step_r, step_c = 64, 256

    def weigh(i, h, w_ref):
        ar = jnp.transpose(ral[i, h])[:, 0:1]
        for r in range(own // step_r):
            a_r = jnp.broadcast_to(ar[r * step_r : (r + 1) * step_r], (step_r, 128))
            a_r = jnp.concatenate([a_r] * (step_c // 128), axis=1)
            c_r = rc[i, h * own + r * step_r : h * own + (r + 1) * step_r, :]
            c_r = jnp.concatenate([c_r] * (step_c // 128), axis=1)
            for c in range(every // step_c):
                sl = slice(c * step_c, (c + 1) * step_c)
                d = t_ref[i, h * own + r * step_r : h * own + (r + 1) * step_r, sl]
                v = jnp.exp2(d * c_r) * a_r + jnp.exp2(d * cv[0:1, sl]) * cv[1:2, sl]
                w_ref[r * step_r : (r + 1) * step_r, sl] = v.astype(BF16)

    def order(j):
        return 7 - j - 2 * (j == 4).astype(jnp.int32) + ((j == 5) | (j == 6)).astype(jnp.int32)

    def to_sibling(i):
        return remote(
            t_ref.at[i, pl.ds(own, own), pl.ds(0, feats)], sr.at[i], sr_s.at[i], sr_r.at[i], rpeer(0, 0, 1)
        )

    def to_owner(i):
        dx, e = pick(i, [p[0] for p in PLACES]), pick(i, [p[1] for p in PLACES])
        b = pick(i, BACK)
        return remote(ob.at[i], obr.at[b], ob_s.at[i], ob_r.at[b], rpeer(dx, 4 - e, 0))

    def finish(j):
        i = order(j)
        arrived(sr.at[i], sr_r.at[i])
        ob[i] = (sr[i] + mn[j % 2]).astype(BF16)
        to_owner(i).start()

    def out_step(j, carry):
        i = order(j)
        for h in (1, 0):
            @pl.when(i + h > 0)
            def _():
                arrived(ral.at[i, h], ral_r.at[i, h])
        everything = fb[...].reshape(every, feats)
        weigh(i, 1, w1)
        mn[(j + 1) % 2] = jnp.dot(w0[...], everything, preferred_element_type=F32)

        @pl.when(j >= 2)
        def _():
            finish(j - 2)

        other = jnp.dot(w1[...], everything, preferred_element_type=F32)
        weigh(i, 0, w0)
        t_ref[i, own : 2 * own, 0:feats] = other
        to_sibling(i).start()
        return carry

    lax.fori_loop(0, 8, out_step, 0)
    finish(jnp.int32(6) + row * 0)
    result = jnp.dot(w0[...], fb[...].reshape(every, feats), preferred_element_type=F32)
    arrived(sr.at[0], sr_r.at[0])
    result = result + sr[0]
    for i in (7, 6, 5, 4, 1, 3, 2):
        arrived(obr.at[i], ob_r.at[i])
        result = result + obr[i].astype(F32)
    out_ref[...] = result
    for make in started:
        remote(*make()).wait_send()

    def drain(i, carry):
        to_sibling(i).wait_send()

        @pl.when(i > 0)
        def _():
            to_owner(i).wait_send()
        return carry

    lax.fori_loop(0, 8, drain, 0)


def shards(embeddings, spread, features, block_list, list_pairs):
    own, wide = embeddings.shape
    feats = features.shape[1]
    rate = jnp.broadcast_to(spread.astype(F32)[None] * (-2.0 * LOG2E), (8, own))
    anywhere = pl.BlockSpec(memory_space=pl.ANY)
    scalars = pl.BlockSpec(memory_space=pltpu.SMEM)
    whole = pl.BlockSpec(memory_space=pltpu.VMEM)
    vmem, dma = pltpu.VMEM, pltpu.SemaphoreType.DMA
    return pl.pallas_call(
        kernel,
        out_shape=jax.ShapeDtypeStruct((own, feats), F32),
        in_specs=[anywhere] * 2 + [whole] + [scalars] * 2,
        out_specs=whole,
        scratch_shapes=[
            vmem((8, 2, own, wide), BF16),
            vmem((8, own, wide), BF16),
            vmem((8, own, feats), BF16),
            vmem((8, 2 * own, 8 * own), F32),
            vmem((8, 2 * own, 128), F32),
            vmem((8, 2 * own, 128), F32),
            vmem((8, 2, 8, own), F32),
            vmem((8, 8, own), F32),
            vmem((8, 8, own), F32),
            vmem((8, 8, own), F32),
            vmem((8, own), F32),
            vmem((8, 2, 8, own), F32),
            vmem((8, 8, own), F32),
            vmem((8, 8 * own), F32),
            vmem((own, 8 * own), BF16),
            vmem((own, 8 * own), BF16),
            vmem((2, own, feats), F32),
            vmem((8, own, feats), F32),
            vmem((8, own, feats), BF16),
            vmem((8, own, feats), BF16),
            pltpu.SMEM((32,), jnp.int32),
            pltpu.SMEM((16,), jnp.int32),
            dma((3,)),
            dma((9, 2)), dma((8, 3)), dma((8, 2)), dma((8, 2)),
            dma((9, 2)), dma((8, 3)), dma((9, 2)), dma((8, 3)),
            dma((8,)), dma((8,)),
            dma((8, 3)), dma((8, 2)), dma((8,)),
            dma((8,)), dma((8,)), dma((8,)), dma((8,)),
        ],
        compiler_params=pltpu.CompilerParams(
            collective_id=0, has_side_effects=True, vmem_limit_bytes=61 * 2**20
        ),
        name="affinities",
    )(embeddings, features, rate, block_list, list_pairs)


def solution(mesh):
    return jax.shard_map(
        shards,
        mesh=mesh,
        in_specs=(P(("row", "col"), None), P(("row", "col")), P(("row", "col"), None), P(), P()),
        out_specs=P(("row", "col"), None),
        check_vma=False,
    )
```

time: 549 us -> 84.6 us (0.15)
  waiting for transfers between devices: 193 us -> 0 us
  blocking collectives: 112 us -> 0 us
  matrix products: 109 us -> 0 us
  Pallas kernels: 0 us -> 81.2 us
  loops' own time: 57.7 us -> 0 us
  local copies, waits for them, and re-layouts: 54 us -> 2.27 us
  between operations: 13.2 us -> 0.01 us
  other arithmetic: 8.3 us -> 0.66 us
    psum x1 -> x0, waiting for transfers between devices: 130 us -> none  [shards(): summed = lax.psum(partial_out, 'col')]
    dot_general x20 -> x0, matrix products: 109 us -> none  [the longest x8 61 us: one_block(): return jnp.dot(weight, cols_feat, preferred_element_type=jnp.float32)]
    pallas_call x0 -> x1, Pallas kernels: none -> 81.2 us  [shards(): pl.pallas_call(kernel, out_shape=jax.ShapeDtypeStruct((own, feats), F32),...]
    all_gather x3 -> x0, blocking collectives: 61.1 us -> none  [the longest x1 21.2 us: shards(): lax.all_gather(spread, 'col', axis=0, tiled=True)]
    all_gather x3 -> x0, waiting for transfers between devices: 60.8 us -> none  [the longest x1 39.8 us: shards(): lax.all_gather(embeddings, 'col', axis=0, tiled=True)]
    another operation x2 -> x0, loops' own time: 57.7 us -> none  [the longest x1 30.1 us: shards(): lax.map(lambda start: jnp.sum(block_terms(start, block_rows)[2], axis=1),...]
    psum x1 -> x0, blocking collectives: 51.3 us -> none  [shards(): row_totals = lax.psum(row_partial, 'col')]
    broadcast_in_dim x16 -> x1, local copies, waits for them, and re-layouts: 38.6 us -> 0.6 us  [shards(): rate = jnp.broadcast_to(spread.astype(F32)[None] * (-2.0 * LOG2E), (8, own))]
  transfers between devices with their start and end apart: 4 -> 0, of which waited for: 3 -> 0; matrix products, arithmetic and copies ran while one was open for 15% -> 0% of each run, Pallas kernels for 0% -> 0%
where the time goes in v2:
time: 84.6 us; the launch traced here: 84.2 us
  Pallas kernels  81.2 us (96%)
  local copies, waits for them, and re-layouts  2.27 us (3%)
    pallas_call x1, Pallas kernels, shards(): pl.pallas_call(kernel, out_shape=jax.ShapeDtypeStruct((own, feats), F32),...  81.2 us

profile of v2, /device:TPU:1, one launch (start us, length us, event | category | flops | bytes accessed | tf_op | source)
XLA Modules:
  0.0 84.2 jit_solution(1173785857110098186)
XLA Ops:
  0.0 0.7 convert_multiply_fusion
  0.7 0.6 broadcast_in_dim.2.rate_ref
  1.3 81.2 %affinities.1 = f32[256,256]{1,0:T(8,128)} custom-call(bf16[256,768]{1,0:T(8,128)(2,1)} %x_ref.1, bf16[256,256]{1,0:T(8,128)(2,1)} %f_ref.1, f32[8,256]{1,0:T(8,128)} %broadcast_in_dim.2.rate_ref, s32[256]{0:T(256)} %bl_ref.1, s32[64,64]{1,0:T(8,128)} %lp_ref.1), custom_call_target="tpu_custom_call" | custom-call | tf_op jit(solution)/shard_map/affinities/pallas_call | solution.py:368
  82.5 1.7 %copy.7 = f32[256,256]{1,0:T(8,128)} copy(f32[256,256]{1,0:T(8,128)} %affinities.1) | data formatting | bytes 524288

commit v3 on v2

--- a/solution.py
+++ b/solution.py
@@ -14,8 +14,9 @@
 INF = float("inf")
 MESH = pl.DeviceIdType.MESH
 
-PLACES = ((0, 0), (1, 0), (0, 1), (0, 3), (1, 1), (1, 3), (0, 2), (1, 2))
+PLACES = ((0, 0), (1, 0), (0, 1), (0, 3), (0, 2), (1, 1), (1, 3), (1, 2))
 SLOT = {p: s for s, p in enumerate(PLACES)}
+ORDER = (0, 7, 4, 5, 6, 1, 3, 2)
 BACK = [SLOT[(dx, (4 - e) % 4)] for dx, e in PLACES]
 RECTS = ((0, 2, 0, 2), (2, 1, 0, 2), (0, 3, 2, 1), (3, 1, 0, 3), (0, 4, 3, 1))
 
@@ -26,9 +27,9 @@
 
 def kernel(
     x_ref, f_ref, rate_ref, bl_ref, lp_ref, out_ref,
-    rx, cx, fb, t_ref, rn, rc, ra, ca, cs, tr, al, ral, cal, cv, w0, w1, mn, sr, ob, obr, rl, cl,
+    rx, cx, fb, t_ref, rn, rc, ra, ca, cs, tr, al, ral, cm, cv, w0, mn, sr, ob, obr, rl, cl,
     loc, rx_s, rx_r, dd_s, dd_r, cx_s, cx_r, fb_s, fb_r, tr_s, tr_r,
-    al_s, ral_r, cal_r, sr_s, sr_r, ob_s, ob_r,
+    al_s, ral_r, sr_s, sr_r, ob_s, ob_r,
 ):
     own, wide = x_ref.shape
     feats = f_ref.shape[1]
@@ -70,7 +71,6 @@
         for b in range(2):
             cl[i * 2 + b] = bl_ref[owner * 2 + b]
     cs[...] = jnp.zeros_like(cs)
-    w0[...] = jnp.zeros_like(w0)
 
     for c in locals_:
         c.wait()
@@ -109,17 +109,31 @@
             if self.side is not None and part != 1:
                 send(lambda: (self.side(a), self.side(b), self.ssem.at[m, 1], self.rsem.at[b, 2], self.peer(*to)))
 
-        def own_x(self):
-            self.move(0, 0, 1, None, (1, 0))
-
-        def ring(self, dx):
-            base = SLOT[(dx, 0)]
-            self.move(1 + 4 * dx, base, SLOT[(dx, 1)], None, (0, 1))
-            self.move(2 + 4 * dx, base, SLOT[(dx, 3)], None, (0, -1))
-
-        def halves(self, dx):
-            self.move(3 + 4 * dx, SLOT[(dx, 1)], SLOT[(dx, 2)], 0, (0, 1))
-            self.move(4 + 4 * dx, SLOT[(dx, 3)], SLOT[(dx, 2)], 1, (0, -1))
+        def first(self):
+            self.move(1, 0, SLOT[(0, 1)], None, (0, 1))
+            self.move(2, 0, SLOT[(0, 3)], None, (0, -1))
+            self.move(0, 0, SLOT[(1, 0)], None, (1, 0))
+
+        def second(self):
+            self.recv(SLOT[(0, 1)])
+            self.recv(SLOT[(0, 3)])
+            self.move(3, SLOT[(0, 1)], SLOT[(0, 2)], 0, (0, 1))
+            self.move(4, SLOT[(0, 3)], SLOT[(0, 2)], 1, (0, -1))
+            self.move(6, SLOT[(0, 1)], SLOT[(1, 1)], None, (1, 0))
+            self.recv(SLOT[(1, 0)])
+            self.move(5, SLOT[(1, 0)], SLOT[(1, 3)], None, (0, -1))
+
+        def third(self):
+            self.recv(SLOT[(0, 2)])
+            self.move(7, SLOT[(0, 2)], SLOT[(1, 2)], 0, (1, 0))
+
+        def fourth(self):
+            self.recv(SLOT[(1, 1)])
+            self.move(8, SLOT[(1, 1)], SLOT[(1, 2)], 1, (0, 1))
+
+        def last(self):
+            self.recv(SLOT[(1, 3)])
+            self.recv(SLOT[(1, 2)])
 
         def recv(self, slot):
             if PLACES[slot][1] == 2:
@@ -182,56 +196,38 @@
         for c in range(2):
             cs[2 * qi + c] = cs[2 * qi + c] + jnp.concatenate(acc[c * per : (c + 1) * per], axis=1)
 
-    def give_sum(q):
-        dx, e = PLACES[q]
-        send(lambda: (cs.at[q], tr.at[BACK[q]], tr_s.at[q], tr_r.at[BACK[q]], cpeer(dx, -e)))
-
-    rows.ring(0)
-    cols.ring(0)
-    rows.own_x()
-    cols.own_x()
+    rows.first()
+    cols.first()
     sibling(0)
     row_ready(0)
 
     def before(k):
         if k == 0:
-            for g in (rows, cols):
-                g.recv(1)
-                g.ring(1)
-                g.recv(2)
-                g.recv(3)
-                g.halves(0)
+            rows.second()
+            cols.second()
             for s in (1, 2, 3):
                 sibling(s)
             for s in (1, 2, 3):
                 row_ready(s)
         if k == 1:
-            for g in (rows, cols):
-                g.recv(4)
-                g.recv(5)
-                g.halves(1)
+            rows.third()
+            cols.third()
+            rows.fourth()
+            cols.fourth()
+            feat.first()
             for s in (4, 5):
                 sibling(s)
-            feat.ring(0)
-            feat.own_x()
             for s in (4, 5):
                 row_ready(s)
         if k == 3:
+            rows.last()
             for s in (6, 7):
-                rows.recv(s)
                 sibling(s)
+            cols.last()
             for s in (6, 7):
                 row_ready(s)
         if k == 4:
-            for s in (6, 7):
-                cols.recv(s)
-            for q in range(1, 6):
-                give_sum(q)
-            feat.recv(1)
-            feat.ring(1)
-            feat.recv(2)
-            feat.recv(3)
-            feat.halves(0)
+            feat.second()
 
     def rect(k, carry):
         first, count_r, lead, count_c = (pick(k, [r[f] for r in RECTS]) for f in range(4))
@@ -251,52 +247,53 @@
 
     lax.fori_loop(0, len(RECTS), rect, 0)
 
-    give_sum(6)
-    give_sum(7)
-    feat.recv(4)
-    feat.recv(5)
-    feat.halves(1)
-    total = cs[0]
-    for q in range(1, 8):
-        arrived(tr.at[q], tr_r.at[q])
-        total = total + tr[q]
-    al[...] = jnp.broadcast_to(0.5 / jnp.sum(total, axis=0, keepdims=True), al.shape)
+    for q in range(8):
+        cm[q : q + 1, :] = jnp.sum(cs[q], axis=0, keepdims=True)
+    for s in range(1, 8):
+        dx, e = PLACES[s]
+        send(lambda s=s, dx=dx, e=e: (cm, tr.at[s], tr_s.at[s], tr_r.at[s], cpeer(dx, e)))
+    feat.third()
+    feat.fourth()
+    for s in range(1, 8):
+        arrived(tr.at[s], tr_r.at[s])
+
+    def factor(q):
+        total = cm[q : q + 1, :]
+        for s in range(1, 8):
+            p = SLOT[((PLACES[q][0] + PLACES[s][0]) % 2, (PLACES[q][1] - PLACES[s][1]) % 4)]
+            total = total + tr[s, p : p + 1, :]
+        return 0.5 / total
+
+    al[...] = jnp.broadcast_to(factor(0), al.shape)
     ral[0, 0] = al[...]
-    cal[0] = al[...]
-    for i in (7, 6, 5, 4, 1, 3, 2, 0):
-        dx, e = PLACES[i]
-        if i > 0:
-            send(lambda i=i, dx=dx, e=e: (al, cal.at[i], al_s.at[i, 2], cal_r.at[i], cpeer(dx, e)))
-    for i in (7, 6, 5, 4, 1, 3, 2, 0):
+    for i in ORDER:
         dx, e = PLACES[i]
         for h in (1, 0):
             if i + h > 0:
                 send(lambda i=i, h=h, dx=dx, e=e: (al, ral.at[i, h], al_s.at[i, h], ral_r.at[i, h], rpeer(dx, e, h)))
     for q in range(8):
-        if q > 0:
-            arrived(cal.at[q], cal_r.at[q])
         cv[0:1, q * own : (q + 1) * own] = ca[q, 1:2, :]
-        cv[1:2, q * own : (q + 1) * own] = cal[q, 0:1, :]
-
-    feat.recv(6)
-    feat.recv(7)
+        cv[1:2, q * own : (q + 1) * own] = al[0:1, :] if q == 0 else factor(q)
+    feat.last()
     step_r, step_c = 64, 256
 
-    def weigh(i, h, w_ref):
-        ar = jnp.transpose(ral[i, h])[:, 0:1]
-        for r in range(own // step_r):
-            a_r = jnp.broadcast_to(ar[r * step_r : (r + 1) * step_r], (step_r, 128))
+    def weigh(i, w_ref):
+        for r in range(2 * own // step_r):
+            if r * step_r % own == 0:
+                ar = jnp.transpose(ral[i, r * step_r // own])[:, 0:1]
+            lo = r * step_r % own
+            a_r = jnp.broadcast_to(ar[lo : lo + step_r], (step_r, 128))
             a_r = jnp.concatenate([a_r] * (step_c // 128), axis=1)
-            c_r = rc[i, h * own + r * step_r : h * own + (r + 1) * step_r, :]
-            c_r = jnp.concatenate([c_r] * (step_c // 128), axis=1)
+            at = slice(r * step_r, (r + 1) * step_r)
+            c_r = jnp.concatenate([rc[i, at, :]] * (step_c // 128), axis=1)
             for c in range(every // step_c):
                 sl = slice(c * step_c, (c + 1) * step_c)
-                d = t_ref[i, h * own + r * step_r : h * own + (r + 1) * step_r, sl]
+                d = t_ref[i, at, sl]
                 v = jnp.exp2(d * c_r) * a_r + jnp.exp2(d * cv[0:1, sl]) * cv[1:2, sl]
-                w_ref[r * step_r : (r + 1) * step_r, sl] = v.astype(BF16)
+                w_ref[at, sl] = v.astype(BF16)
 
     def order(j):
-        return 7 - j - 2 * (j == 4).astype(jnp.int32) + ((j == 5) | (j == 6)).astype(jnp.int32)
+        return pick(j, ORDER)
 
     def to_sibling(i):
         return remote(
@@ -307,6 +304,10 @@
         dx, e = pick(i, [p[0] for p in PLACES]), pick(i, [p[1] for p in PLACES])
         b = pick(i, BACK)
         return remote(ob.at[i], obr.at[b], ob_s.at[i], ob_r.at[b], rpeer(dx, 4 - e, 0))
+
+    def give_sibling(i, part):
+        t_ref[i, own : 2 * own, 0:feats] = part
+        to_sibling(i).start()
 
     def finish(j):
         i = order(j)
@@ -314,32 +315,41 @@
         ob[i] = (sr[i] + mn[j % 2]).astype(BF16)
         to_owner(i).start()
 
-    def out_step(j, carry):
-        i = order(j)
-        for h in (1, 0):
+    def await_factors(i):
+        for h in range(2):
             @pl.when(i + h > 0)
             def _():
                 arrived(ral.at[i, h], ral_r.at[i, h])
-        everything = fb[...].reshape(every, feats)
-        weigh(i, 1, w1)
-        mn[(j + 1) % 2] = jnp.dot(w0[...], everything, preferred_element_type=F32)
-
-        @pl.when(j >= 2)
+
+    def multiply(w_ref):
+        return jnp.dot(w_ref[...], fb[...].reshape(every, feats), preferred_element_type=F32)
+
+    def hand_out(j, part):
+        i = order(j)
+        give_sibling(i, part[own:])
+        mn[j % 2] = part[:own]
+
+        @pl.when(j == 0)
         def _():
-            finish(j - 2)
-
-        other = jnp.dot(w1[...], everything, preferred_element_type=F32)
-        weigh(i, 0, w0)
-        t_ref[i, own : 2 * own, 0:feats] = other
-        to_sibling(i).start()
+            t_ref[0, 0:own, 0:feats] = part[:own]
+
+        @pl.when(j > 1)
+        def _():
+            finish(j - 1)
+
+    def out_step(j, carry):
+        i = order(j)
+        await_factors(i)
+        weigh(i, w0)
+        hand_out(j, multiply(w0))
         return carry
 
     lax.fori_loop(0, 8, out_step, 0)
-    finish(jnp.int32(6) + row * 0)
-    result = jnp.dot(w0[...], fb[...].reshape(every, feats), preferred_element_type=F32)
+    finish(row * 0 + 7)
+    result = t_ref[0, 0:own, 0:feats]
     arrived(sr.at[0], sr_r.at[0])
     result = result + sr[0]
-    for i in (7, 6, 5, 4, 1, 3, 2):
+    for i in ORDER[1:]:
         arrived(obr.at[i], ob_r.at[i])
         result = result + obr[i].astype(F32)
     out_ref[...] = result
@@ -383,10 +393,9 @@
             vmem((8, 8, own), F32),
             vmem((8, own), F32),
             vmem((8, 2, 8, own), F32),
-            vmem((8, 8, own), F32),
+            vmem((8, own), F32),
             vmem((8, 8 * own), F32),
-            vmem((own, 8 * own), BF16),
-            vmem((own, 8 * own), BF16),
+            vmem((2 * own, 8 * own), BF16),
             vmem((2, own, feats), F32),
             vmem((8, own, feats), F32),
             vmem((8, own, feats), BF16),
@@ -397,7 +406,7 @@
             dma((9, 2)), dma((8, 3)), dma((8, 2)), dma((8, 2)),
             dma((9, 2)), dma((8, 3)), dma((9, 2)), dma((8, 3)),
             dma((8,)), dma((8,)),
-            dma((8, 3)), dma((8, 2)), dma((8,)),
+            dma((8, 2)), dma((8, 2)),
             dma((8,)), dma((8,)), dma((8,)), dma((8,)),
         ],
         compiler_params=pltpu.CompilerParams(

time: 84.6 us -> 79.8 us (0.943)
  Pallas kernels: 81.2 us -> 76.6 us
    pallas_call x1, Pallas kernels: 81.2 us -> 76.6 us  [shards(): pl.pallas_call(kernel, out_shape=jax.ShapeDtypeStruct((own, feats), F32),...]
where the time goes in v3:
time: 79.8 us; the launch traced here: 79.5 us
  Pallas kernels  76.6 us (96%)
  local copies, waits for them, and re-layouts  2.27 us (3%)
    pallas_call x1, Pallas kernels, shards(): pl.pallas_call(kernel, out_shape=jax.ShapeDtypeStruct((own, feats), F32),...  76.6 us
    unnamed x1, local copies, waits for them, and re-layouts  1.67 us

profile of v3, /device:TPU:1, one launch (start us, length us, event | category | flops | bytes accessed | tf_op | source)
XLA Modules:
  0.0 79.5 jit_solution(10323443538843068382)
XLA Ops:
  0.0 0.7 convert_multiply_fusion
  0.7 0.6 broadcast_in_dim.2.rate_ref
  1.3 76.6 %affinities.1 = f32[256,256]{1,0:T(8,128)} custom-call(bf16[256,768]{1,0:T(8,128)(2,1)} %x_ref.1, bf16[256,256]{1,0:T(8,128)(2,1)} %f_ref.1, f32[8,256]{1,0:T(8,128)} %broadcast_in_dim.2.rate_ref, s32[256]{0:T(256)} %bl_ref.1, s32[64,64]{1,0:T(8,128)} %lp_ref.1), custom_call_target="tpu_custom_call" | custom-call | tf_op jit(solution)/shard_map/affinities/pallas_call | solution.py:378
  77.9 1.7 %copy.7 = f32[256,256]{1,0:T(8,128)} copy(f32[256,256]{1,0:T(8,128)} %affinities.1) | data formatting | bytes 524288

commit v4 on v3

--- a/solution.py
+++ b/solution.py
@@ -16,7 +16,7 @@
 
 PLACES = ((0, 0), (1, 0), (0, 1), (0, 3), (0, 2), (1, 1), (1, 3), (1, 2))
 SLOT = {p: s for s, p in enumerate(PLACES)}
-ORDER = (0, 7, 4, 5, 6, 1, 3, 2)
+ORDER = (0, 4, 7, 6, 5, 1, 2, 3)
 BACK = [SLOT[(dx, (4 - e) % 4)] for dx, e in PLACES]
 RECTS = ((0, 2, 0, 2), (2, 1, 0, 2), (0, 3, 2, 1), (3, 1, 0, 3), (0, 4, 3, 1))
 
@@ -78,7 +78,8 @@
     norm = jnp.sum(xf * xf, axis=1, keepdims=True) * 0.5
     norm = jnp.transpose(jnp.broadcast_to(norm, (own, 128)))
     ra[0, 0, 0:1, :] = norm[0:1, :]
-    ra[0, 0, 1:8, :] = rate_ref[1:8, :]
+    rate = rate_ref[...].astype(F32).reshape(1, own) * (-2.0 * LOG2E)
+    ra[0, 0, 1:8, :] = jnp.broadcast_to(rate, (7, own))
     ca[0] = ra[0, 0]
 
     pl.semaphore_wait(barrier, len(met))
@@ -204,19 +205,19 @@
     def before(k):
         if k == 0:
             rows.second()
-            cols.second()
             for s in (1, 2, 3):
                 sibling(s)
+            cols.second()
             for s in (1, 2, 3):
                 row_ready(s)
         if k == 1:
             rows.third()
+            sibling(4)
             cols.third()
             rows.fourth()
+            sibling(5)
             cols.fourth()
             feat.first()
-            for s in (4, 5):
-                sibling(s)
             for s in (4, 5):
                 row_ready(s)
         if k == 3:
@@ -370,7 +371,6 @@
 def shards(embeddings, spread, features, block_list, list_pairs):
     own, wide = embeddings.shape
     feats = features.shape[1]
-    rate = jnp.broadcast_to(spread.astype(F32)[None] * (-2.0 * LOG2E), (8, own))
     anywhere = pl.BlockSpec(memory_space=pl.ANY)
     scalars = pl.BlockSpec(memory_space=pltpu.SMEM)
     whole = pl.BlockSpec(memory_space=pltpu.VMEM)
@@ -413,7 +413,7 @@
             collective_id=0, has_side_effects=True, vmem_limit_bytes=61 * 2**20
         ),
         name="affinities",
-    )(embeddings, features, rate, block_list, list_pairs)
+    )(embeddings, features, spread, block_list, list_pairs)
 
 
 def solution(mesh):

time: 79.8 us -> 76.9 us (0.964)
  Pallas kernels: 76.6 us -> 75 us
    pallas_call x1, Pallas kernels: 76.6 us -> 75 us  [shards(): pl.pallas_call(kernel, out_shape=jax.ShapeDtypeStruct((own, feats), F32),...]
where the time goes in v4:
time: 76.9 us; the launch traced here: 76.6 us
  Pallas kernels  75 us (98%)
  local copies, waits for them, and re-layouts  1.67 us (2%)
    pallas_call x1, Pallas kernels, shards(): pl.pallas_call(kernel, out_shape=jax.ShapeDtypeStruct((own, feats), F32),...  75 us
    unnamed x1, local copies, waits for them, and re-layouts  1.67 us

profile of v4, /device:TPU:1, one launch (start us, length us, event | category | flops | bytes accessed | tf_op | source)
XLA Modules:
  0.0 76.6 jit_solution(6483621814698932370)
XLA Ops:
  0.0 75.0 %affinities.1 = f32[256,256]{1,0:T(8,128)} custom-call(bf16[256,768]{1,0:T(8,128)(2,1)} %x_ref.1, bf16[256,256]{1,0:T(8,128)(2,1)} %f_ref.1, bf16[256]{0:T(256)(128)(2,1)} %rate_ref.1, s32[256]{0:T(256)} %bl_ref.1, s32[64,64]{1,0:T(8,128)} %lp_ref.1), custom_call_target="tpu_custom_call" | custom-call | tf_op jit(solution)/shard_map/affinities/pallas_call | solution.py:378
  75.0 1.7 %copy.7 = f32[256,256]{1,0:T(8,128)} copy(f32[256,256]{1,0:T(8,128)} %affinities.1) | data formatting | bytes 524288

commit v5 on v4

--- a/solution.py
+++ b/solution.py
@@ -18,7 +18,7 @@
 SLOT = {p: s for s, p in enumerate(PLACES)}
 ORDER = (0, 4, 7, 6, 5, 1, 2, 3)
 BACK = [SLOT[(dx, (4 - e) % 4)] for dx, e in PLACES]
-RECTS = ((0, 2, 0, 2), (2, 1, 0, 2), (0, 3, 2, 1), (3, 1, 0, 3), (0, 4, 3, 1))
+RECTS = ((0, 2, 0, 2), (2, 1, 0, 2), (0, 3, 2, 1), (0, 3, 3, 1), (3, 1, 0, 4))
 
 
 def pick(i, values):
@@ -72,8 +72,7 @@
             cl[i * 2 + b] = bl_ref[owner * 2 + b]
     cs[...] = jnp.zeros_like(cs)
 
-    for c in locals_:
-        c.wait()
+    locals_[0].wait()
     xf = rx[0, 0].astype(F32)
     norm = jnp.sum(xf * xf, axis=1, keepdims=True) * 0.5
     norm = jnp.transpose(jnp.broadcast_to(norm, (own, 128)))
@@ -81,6 +80,8 @@
     rate = rate_ref[...].astype(F32).reshape(1, own) * (-2.0 * LOG2E)
     ra[0, 0, 1:8, :] = jnp.broadcast_to(rate, (7, own))
     ca[0] = ra[0, 0]
+    for c in locals_[1:]:
+        c.wait()
 
     pl.semaphore_wait(barrier, len(met))
 
@@ -225,9 +226,9 @@
             for s in (6, 7):
                 sibling(s)
             cols.last()
+        if k == 4:
             for s in (6, 7):
                 row_ready(s)
-        if k == 4:
             feat.second()
 
     def rect(k, carry):

time: 76.9 us -> 75.6 us (0.983)
  Pallas kernels: 75 us -> 73.7 us
    pallas_call x1, Pallas kernels: 75 us -> 73.7 us  [shards(): pl.pallas_call(kernel, out_shape=jax.ShapeDtypeStruct((own, feats), F32),...]
where the time goes in v5:
time: 75.6 us; the launch traced here: 75.4 us
  Pallas kernels  73.7 us (97%)
  local copies, waits for them, and re-layouts  1.67 us (2%)
    pallas_call x1, Pallas kernels, shards(): pl.pallas_call(kernel, out_shape=jax.ShapeDtypeStruct((own, feats), F32),...  73.7 us
    unnamed x1, local copies, waits for them, and re-layouts  1.67 us

profile of v5, /device:TPU:1, one launch (start us, length us, event | category | flops | bytes accessed | tf_op | source)
XLA Modules:
  0.0 75.4 jit_solution(3314324394494138414)
XLA Ops:
  0.0 73.7 %affinities.1 = f32[256,256]{1,0:T(8,128)} custom-call(bf16[256,768]{1,0:T(8,128)(2,1)} %x_ref.1, bf16[256,256]{1,0:T(8,128)(2,1)} %f_ref.1, bf16[256]{0:T(256)(128)(2,1)} %rate_ref.1, s32[256]{0:T(256)} %bl_ref.1, s32[64,64]{1,0:T(8,128)} %lp_ref.1), custom_call_target="tpu_custom_call" | custom-call | tf_op jit(solution)/shard_map/affinities/pallas_call | solution.py:379
  73.7 1.7 %copy.7 = f32[256,256]{1,0:T(8,128)} copy(f32[256,256]{1,0:T(8,128)} %affinities.1) | data formatting | bytes 524288
